TPU v7x, 128 devices: a whole 4x4x4 slice. The times are simulated.
128 devices in a mesh: req: 8 (over y, z_hi), mlp: 16 (over z_lo, x, core).
Axes of the slice: x: 4, y: 4, z: 4 (z_hi: 2, z_lo: 2; z = z_hi * 2 + z_lo), core: 2. Of those that a mesh axis runs over, the one named last changes fastest.
Arguments:
- prompt_tokens: bfloat16 [16, 1024, 2048], P('req', None, 'mlp'), may hold values from -6 to 6
- decode_tokens: bfloat16 [32, 2048], P('req', 'mlp'), may hold values from -6 to 6
- prompt_lengths: int32 [16], P('req'), may hold values from 128 to 1024, as said below
- decode_states: float32 [32, 16, 128, 128], P('req', 'mlp'), may hold values from -6 to 6
- w_fio: float32 [2048, 6144], P('req', 'mlp'), may hold values from -0.125 to 0.125
- forget_bias: float32 [2048], P('mlp'), as said below
- head_gain: float32 [2048], P('mlp'), may hold values from 0.1 to 1.9
- w_out: float32 [2048, 2048], P('mlp', 'req'), may hold values from -0.125 to 0.125
- mlp_gain: float32 [2048], replicated, may hold values from 0.1 to 1.9
- w_gu: float32 [2048, 11264], P('req', 'mlp'), may hold values from -0.125 to 0.125
- w_down: float32 [5632, 2048], P('mlp', 'req'), may hold values from -0.078125 to 0.078125
Outputs:
- prompt_out: bfloat16 [16, 1024, 2048], P('req', None, 'mlp')
- decode_out: bfloat16 [32, 2048], P('req', 'mlp')
- prompt_states: float32 [16, 16, 128, 128], P('req', 'mlp')
- decode_next: float32 [32, 16, 128, 128], P('req', 'mlp')
Inputs may be any that keep to these rules, and one draw needn't show every extreme that they name: `prompt_lengths`: slots at or past a prompt's length are padding; one prompt has length 1024 and another 1024 // 8. `forget_bias`: every entry is at least 3 and at most ln(1024) + 1.7.
All inputs are finite; a program needn't handle non-finite values.
Results may differ from a plain program's by a relative error of at most 0.02.
Values may be sent and summed in bfloat16 or wider, within the bound.
No kernel may reach another device: no remote copies, remote signals or barrier semaphores. Data moves between devices by JAX's collectives and lax.ppermute only.
A program may use at most 128 MiB of HBM per device.

v0:
```python
import jax
import jax.numpy as jnp
from jax import lax
from jax.sharding import PartitionSpec as P

BLOCK = 64
epsilon = 1e-05


def add_columns(operand, weights_piece):
    return jnp.dot(operand, weights_piece, preferred_element_type=jnp.float32)


def project_output(source_rows, weights):
    return jnp.dot(
        source_rows,
        lax.all_gather(weights, "req", axis=1, tiled=True),
        preferred_element_type=jnp.float32,
    )


def block_step(carried, forget_block, value_block, query_block, start_row, lengths):
    steps_here = forget_block.shape[1]
    positions = start_row + jnp.arange(steps_here, dtype=jnp.int32)
    alive_mask = (positions[None, :] < lengths[:, None])[:, :, None, None]
    log_forget = jnp.where(alive_mask, jax.nn.log_sigmoid(forget_block), 0.0)
    key_gate = jnp.where(alive_mask, jax.nn.sigmoid(-forget_block), 0.0)
    cumulated = jnp.cumsum(log_forget, axis=1)
    query_tilde = query_block * jnp.exp(cumulated)
    key_tilde = key_gate * jnp.exp(-cumulated)
    scores = jnp.einsum("pthc,pshc->phts", query_tilde, key_tilde, precision=lax.Precision.HIGHEST)
    triangle = jnp.arange(steps_here)[:, None] >= jnp.arange(steps_here)[None, :]
    scores = jnp.where(triangle, scores, 0.0)
    emitted = jnp.einsum("phts,pshv->pthv", scores, value_block, precision=lax.Precision.HIGHEST)
    emitted = emitted + jnp.einsum(
        "pthc,phcv->pthv", query_tilde, carried, precision=lax.Precision.HIGHEST
    )
    emitted = jnp.where(alive_mask, emitted, 0.0)
    last_log = cumulated[:, -1]
    key_decayed = key_gate * jnp.exp(last_log[:, None] - cumulated)
    carried = jnp.exp(last_log)[..., None] * carried + jnp.einsum(
        "pthc,pthv->phcv", key_decayed, value_block, precision=lax.Precision.HIGHEST
    )
    return (carried, emitted)


def on_device(
    prompt_tokens,
    decode_tokens,
    prompt_lengths,
    decode_states,
    w_fio,
    forget_bias,
    head_gain,
    w_out,
    mlp_gain,
    w_gu,
    w_down,
):
    prompts_here, plen, feature_part = prompt_tokens.shape
    heads_here = decode_states.shape[1]
    head_size = decode_states.shape[2]
    prompt_rows = prompts_here * plen
    local_rows = jnp.concatenate(
        [prompt_tokens.reshape(prompt_rows, feature_part), decode_tokens], axis=0
    )
    row_count = local_rows.shape[0]
    x_full = lax.all_gather(local_rows, "mlp", axis=1, tiled=True)
    model_width = x_full.shape[1]
    mixing = add_columns(
        x_full, lax.all_gather(w_fio.astype(jnp.bfloat16), "req", axis=0, tiled=True)
    )
    mixing = mixing.reshape(row_count, heads_here, 3, head_size)
    bias_table = forget_bias.reshape(heads_here, head_size)
    forget_logit = mixing[:, :, 0] + bias_table
    values = mixing[:, :, 1]
    queries = mixing[:, :, 2]
    prompt_forget = forget_logit[:prompt_rows].reshape(prompts_here, plen, heads_here, head_size)
    prompt_values = values[:prompt_rows].reshape(prompts_here, plen, heads_here, head_size)
    prompt_queries = queries[:prompt_rows].reshape(prompts_here, plen, heads_here, head_size)
    start_state = jnp.zeros((prompts_here, heads_here, head_size, head_size), jnp.float32)
    block_total = plen // BLOCK

    def to_blocks(source_array):
        return source_array.reshape(
            prompts_here, block_total, BLOCK, heads_here, head_size
        ).transpose(1, 0, 2, 3, 4)

    def scan_block(carried, inputs):
        forget_block, value_block, query_block, start_row = inputs
        return block_step(
            carried, forget_block, value_block, query_block, start_row, prompt_lengths
        )

    starts = jnp.arange(block_total, dtype=jnp.int32) * BLOCK
    prompt_states, block_outputs = lax.scan(
        scan_block,
        start_state,
        (to_blocks(prompt_forget), to_blocks(prompt_values), to_blocks(prompt_queries), starts),
    )
    prompt_mixed = block_outputs.transpose(1, 0, 2, 3, 4).reshape(
        prompts_here, plen, heads_here, head_size
    )
    decode_logit = forget_logit[prompt_rows:]
    decode_next = (
        jax.nn.sigmoid(decode_logit)[..., None] * decode_states
        + jax.nn.sigmoid(-decode_logit)[..., None] * values[prompt_rows:][:, :, None, :]
    )
    decode_mixed = jnp.einsum(
        "nhcv,nhc->nhv", decode_next, queries[prompt_rows:], precision=lax.Precision.HIGHEST
    )
    mixed_all = jnp.concatenate(
        [prompt_mixed.reshape(prompt_rows, heads_here, head_size), decode_mixed], axis=0
    )
    mean_square = jnp.mean(mixed_all * mixed_all, axis=-1, keepdims=True)
    head_rows = (
        mixed_all * lax.rsqrt(mean_square + epsilon) * head_gain.reshape(heads_here, head_size)
    ).astype(jnp.bfloat16)
    head_rows = head_rows.reshape(row_count, heads_here * head_size)
    offset = lax.axis_index("mlp") * feature_part
    head_terms = project_output(head_rows, w_out.astype(jnp.bfloat16))
    attention = lax.psum_scatter(
        head_terms.astype(jnp.bfloat16), "mlp", scatter_dimension=1, tiled=True
    ).astype(jnp.float32)
    residual = (local_rows.astype(jnp.float32) + attention).astype(jnp.bfloat16)
    residual_wide = residual.astype(jnp.float32)
    square_sum = lax.psum(jnp.sum(residual_wide * residual_wide, axis=1), "mlp")
    row_scale = lax.rsqrt(square_sum / model_width + epsilon)[:, None]
    gain_part = lax.dynamic_slice_in_dim(mlp_gain, offset, feature_part)
    normed_part = (residual_wide * row_scale * gain_part).astype(jnp.bfloat16)
    normed = lax.all_gather(normed_part, "mlp", axis=1, tiled=True)
    gate_up = add_columns(
        normed, lax.all_gather(w_gu.astype(jnp.bfloat16), "req", axis=0, tiled=True)
    )
    hidden_here = w_gu.shape[1] // 2
    hidden = (jax.nn.silu(gate_up[:, :hidden_here]) * gate_up[:, hidden_here:]).astype(jnp.bfloat16)
    down_terms = jnp.dot(
        hidden,
        lax.all_gather(w_down.astype(jnp.bfloat16), "req", axis=1, tiled=True),
        preferred_element_type=jnp.float32,
    )
    down_share = lax.psum_scatter(
        down_terms.astype(jnp.bfloat16), "mlp", scatter_dimension=1, tiled=True
    ).astype(jnp.float32)
    layer_output = (residual_wide + down_share).astype(jnp.bfloat16)
    prompt_out = layer_output[:prompt_rows].reshape(prompts_here, plen, feature_part)
    decode_out = layer_output[prompt_rows:]
    return (prompt_out, decode_out, prompt_states, decode_next)


def solution(mesh):
    placed = (
        P("req", None, "mlp"),
        P("req", "mlp"),
        P("req"),
        P("req", "mlp", None, None),
        P("req", "mlp"),
        P("mlp"),
        P("mlp"),
        P("mlp", "req"),
        P(),
        P("req", "mlp"),
        P("mlp", "req"),
    )
    return jax.shard_map(
        on_device,
        mesh=mesh,
        in_specs=placed,
        out_specs=(
            P("req", None, "mlp"),
            P("req", "mlp"),
            P("req", "mlp", None, None),
            P("req", "mlp", None, None),
        ),
        check_vma=False,
    )
```

profile of v0, /device:TPU:0, one launch (start us, length us, event | category | flops | bytes accessed | tf_op | source)
XLA Modules:
  0.0 637.0 jit_solution(2306237471951861111)
XLA Ops:
  7.2 1.8 convert_element_type.49
  9.1 1.5 pad_maximum_fusion
  10.7 38.0 %all_gather.20 = bf16[128,2048]{1,0:T(8,128)(2,1)} all-gather(bf16[128,256]{1,0:T(8,128)(2,1)S(1)} %convert_element_type.51), channel_id=1, replica_groups=mesh['req'=8,'mlp'=16] {'req'}, dimensions={1}, use_global_device_ids=true | all-gather | bytes 589824 | tf_op jit(solution)/shard_map/all_gather | solution.py:17
  48.7 17.3 %all-gather.8.cloned.1.call-done = bf16[2048,384]{1,0:T(8,128)(2,1)} async-done(((bf16[256,384]{1,0:T(8,128)(2,1)}), bf16[2048,384]{1,0:T(8,128)(2,1)}) %all-gather.8.cloned.1.call-update) | async-done | bytes 1572880 | tf_op jit(solution)/shard_map/all_gather | solution.py:71
  66.1 61.3 %all-gather.6.cloned.1.call-done = bf16[2052,2048]{1,0:T(8,128)(2,1)} async-done(((bf16[2052,128]{1,0:T(8,128)(2,1)}), bf16[2052,2048]{1,0:T(8,128)(2,1)}) %all-gather.6.cloned.1.call-update) | async-done | bytes 8405008 | tf_op jit(solution)/shard_map/all_gather | solution.py:68
  127.4 7.4 %fusion.59 = f32[2052,384]{0,1:T(8,128)S(1)} fusion(bf16[2052,2048]{1,0:T(8,128)(2,1)} %all-gather.6.cloned.1.call-done, bf16[2048,384]{1,0:T(8,128)(2,1)} %all-gather.8.cloned.1.call-done), kind=kOutput, calls=%fused_computation.84 | convolution fusion | flops 3227516928 | bytes 13129728 | tf_op jit(solution)/shard_map/dot_general | solution.py:11
  134.9 1.6 copy-done.3
  137.3 2.2 copy-done.4
  140.8 2.6 copy.47
  143.3 1.3 copy.48
  144.7 108.7 %while.13 = (s32[]{:T(128)}, f32[2,1,128,128]{3,2,0,1:T(8,128)S(1)}, f32[16,2,64,1,128]{4,2,0,1,3:T(8,128)}, s32[16]{0:T(128)S(1)}, s32[2]{0:T(128)S(1)}, /*inde...) while((s32[]{:T(128)}, ...), condition=%wide.region_2.3_spmd.clone, body=%wide.region_0.2_spmd.clone.sunk | while | flops 77050048 | bytes 1596940 | solution.py:96
  148.4 1.7 fusion.93
  150.1 1.3 fusion.91
  155.2 1.7 fusion.93
  162.0 1.7 fusion.93
  163.7 1.3 fusion.91
  168.8 1.7 fusion.93
  170.5 1.3 fusion.91
  175.6 1.7 fusion.93
  177.3 1.3 fusion.91
  182.4 1.7 fusion.93
  184.1 1.3 fusion.91
  189.2 1.7 fusion.93
  190.9 1.3 fusion.91
  196.0 1.7 fusion.93
  197.7 1.3 fusion.91
  202.8 1.7 fusion.93
  209.6 1.7 fusion.93
  216.4 1.7 fusion.93
  223.2 1.7 fusion.93
  229.9 1.7 fusion.93
  236.7 1.7 fusion.93
  243.5 1.7 fusion.93
  250.3 1.7 fusion.93
  254.0 1.6 fusion.49
  255.7 5.6 convolution_convert_fusion.1
  261.3 11.6 %copy.58 = bf16[2052,2048]{0,1:T(8,128)(2,1)} copy(bf16[2052,2048]{1,0:T(8,128)(2,1)} %convolution_convert_fusion.1) | data formatting | bytes 16809984
  275.6 73.2 %reduce-scatter.7.cloned.1.call-done = bf16[128,2052]{1,0:T(8,128)(2,1)} async-done(((bf16[2048,2052]{1,0:T(8,128)(2,1)}), bf16[128,2052]{1,0:T(8,128)(2,1)}) %reduce-scatter.7.cloned.1.call-update) | async-done | bytes 525328
  348.8 1.3 copy.59
  350.5 54.1 %psum.7 = f32[2052]{0:T(1024)S(1)} all-reduce(f32[2052]{0:T(1024)S(1)} %fusion.43), channel_id=1, replica_groups=mesh['req'=8,'mlp'=16] {'mlp'}, use_global_device_ids=true, to_apply=%region_6.7 | all-reduce | flops 2052 | bytes 16416 | tf_op jit(solution)/shard_map/psum | solution.py:127
  406.9 8.9 %all-gather.12.cloned.1.call-done = bf16[2048,704]{0,1:T(8,128)(2,1)} async-done(((bf16[256,704]{0,1:T(8,128)(2,1)}), bf16[2048,704]{0,1:T(8,128)(2,1)}) %all-gather.12.cloned.1.call-update) | async-done | bytes 2883600 | tf_op jit(solution)/shard_map/all_gather | solution.py:133
  415.8 60.6 %all-gather.10.cloned.1.call-done = bf16[2052,2048]{1,0:T(8,128)(2,1)} async-done(((bf16[2052,128]{1,0:T(8,128)(2,1)}), bf16[2052,2048]{1,0:T(8,128)(2,1)}) %all-gather.10.cloned.1.call-update) | async-done | bytes 8405008 | tf_op jit(solution)/shard_map/all_gather | solution.py:131
  476.4 12.6 %fusion.60 = f32[2052,704]{0,1:T(8,128)} fusion(bf16[2052,2048]{1,0:T(8,128)(2,1)} %all-gather.10.cloned.1.call-done, bf16[2048,704]{0,1:T(8,128)(2,1)} %all-gather.12.cloned.1.call-done), kind=kOutput, calls=%fused_computation.85 | convolution fusion | flops 5917114368 | bytes 17067008 | tf_op jit(solution)/shard_map/dot_general | solution.py:11
  489.0 41.2 %all-gather.14.cloned.1.call-done = bf16[352,2048]{1,0:T(8,128)(2,1)} async-done(((bf16[352,256]{1,0:T(8,128)(2,1)}), bf16[352,2048]{1,0:T(8,128)(2,1)}) %all-gather.14.cloned.1.call-update) | async-done | bytes 1441808 | tf_op jit(solution)/shard_map/all_gather | solution.py:139
  530.1 11.1 %convolution_convert_fusion = bf16[2052,2048]{1,0:T(8,128)(2,1)} fusion(bf16[352,2048]{1,0:T(8,128)(2,1)} %all-gather.14.cloned.1.call-done, f32[2052,704]{0,1:T(8,128)} %fusion.60), kind=kOutput, calls=%fused_computation.48 | convolution fusion | flops 2967093504 | bytes 15625216 | tf_op jit(solution)/shard_map/dot_general | solution.py:137
  541.2 11.5 %copy.60 = bf16[2052,2048]{0,1:T(8,128)(2,1)} copy(bf16[2052,2048]{1,0:T(8,128)(2,1)} %convolution_convert_fusion) | data formatting | bytes 16809984
  552.8 74.4 %reduce-scatter.9.cloned.1.call-done = bf16[128,2052]{1,0:T(8,128)(2,1)} async-done(((bf16[2048,2052]{1,0:T(8,128)(2,1)}), bf16[128,2052]{1,0:T(8,128)(2,1)}) %reduce-scatter.9.cloned.1.call-update) | async-done | bytes 525328
  627.2 1.3 copy.61
  (239 shorter events, 80.5 us)
Async XLA Ops:
  7.2 1.9 copy-start
  7.2 3.5 copy-start.11
  7.2 58.9 %all-gather.8.cloned.1.call-start = ((), (), s32[]{:S(2)}) async-start(), calls=%async_computation.3 | async-start | bytes 1769472 | tf_op jit(solution)/shard_map/all_gather | solution.py:71
  9.0 118.4 %all-gather.6.cloned.1.call-start = ((), (), s32[]{:S(2)}) async-start(), calls=%async_computation.2 | async-start | bytes 8947712 | tf_op jit(solution)/shard_map/all_gather | solution.py:68
  10.6 338.2 %reduce-scatter.7.cloned.1.call-start = ((), (), s32[]{:S(2)}) async-start(), calls=%async_computation.7 | async-start | bytes 9469952
  134.8 1.7 copy-start.3
  136.5 0.7 copy-start.14
  137.2 2.3 copy-start.4
  137.3 3.4 copy-start.1
  143.3 1.3 slice-start
  143.3 1.3 copy-start.15
  144.7 108.8 %copy-start.10 = (f32[4,1,128,128]{3,2,1,0:T(8,128)S(1)}, f32[4,1,128,128]{3,2,1,0:T(8,128)}, u32[]{:S(2)}) copy-start(f32[4,1,128,128]{3,2,1,0:T(8,128)} %param.16) | copy-start | bytes 786436
  253.4 7.9 %copy-start.5 = (f32[2,1,128,128]{3,2,0,1:T(8,128)}, f32[2,1,128,128]{3,2,0,1:T(8,128)S(1)}, u32[]{:S(2)}) copy-start(f32[2,1,128,128]{3,2,0,1:T(8,128)S(1)} %get-tuple-element.114) | copy-start | bytes 393220
  253.4 2.3 copy-start.2
  253.4 2.3 copy-start.6
  253.4 2.3 copy-start.13
  253.6 7.7 %copy-start.7 = (f32[4,1,128,128]{3,2,1,0:T(8,128)}, f32[4,1,128,128]{3,2,1,0:T(8,128)S(1)}, u32[]{:S(2)}) copy-start(f32[4,1,128,128]{3,2,1,0:T(8,128)S(1)} %multiply_add_fusion) | copy-start | bytes 786436
  272.9 1.1 copy-start.8
  272.9 77.2 %copy-start.12 = (bf16[4,128]{1,0:T(4,128)(2,1)S(1)}, bf16[4,128]{1,0:T(4,128)(2,1)}, u32[]{:S(2)}) copy-start(bf16[4,128]{1,0:T(4,128)(2,1)} %param.14) | copy-start | bytes 3076
  272.9 142.9 %all-gather.12.cloned.1.call-start = ((), (), s32[]{:S(2)}) async-start(), calls=%async_computation.5 | async-start | bytes 3244032 | tf_op jit(solution)/shard_map/all_gather | solution.py:133
  274.8 201.6 %all-gather.10.cloned.1.call-start = ((), (), s32[]{:S(2)}) async-start(), calls=%async_computation.4 | async-start | bytes 8947712 | tf_op jit(solution)/shard_map/all_gather | solution.py:131
  350.5 55.4 %copy-start.9 = (f32[352,256]{1,0:T(8,128)S(1)}, f32[352,256]{1,0:T(8,128)}, u32[]{:S(2)}) copy-start(f32[352,256]{1,0:T(8,128)} %param.23) | copy-start | bytes 1081348
  405.9 124.3 %all-gather.14.cloned.1.call-start = ((), (), s32[]{:S(2)}) async-start(), calls=%async_computation.6 | async-start | bytes 1622016 | tf_op jit(solution)/shard_map/all_gather | solution.py:139
  406.7 220.6 %reduce-scatter.9.cloned.1.call-start = ((), (), s32[]{:S(2)}) async-start(), calls=%async_computation.8 | async-start | bytes 9469952
Sparse Core Ops, SparseCore 0:
  10.9 55.1 all-gather.7
  67.7 59.6 all-gather.5
  273.0 75.7 reduce-scatter.6
  351.4 64.3 all-gather.11
  417.3 59.0 all-gather.9
  478.4 51.6 all-gather.13
  552.9 74.2 reduce-scatter.8
where the time goes:
time: 641 us; the launch traced here: 637 us
  waiting for transfers between devices  337 us (53%)
  matrix products  121 us (19%)
  blocking collectives  92.2 us (14%)
  local copies, waits for them, and re-layouts  48.2 us (8%)
  other arithmetic  22.7 us (4%)
  between operations  14.4 us (2%)
    unnamed x9, waiting for transfers between devices  148 us
    all_gather x1, waiting for transfers between devices, on_device(): x_full = lax.all_gather(local_rows, 'mlp', axis=1, tiled=True)  61.3 us
    all_gather x1, waiting for transfers between devices, on_device(): normed = lax.all_gather(normed_part, 'mlp', axis=1, tiled=True)  60.6 us
    psum x1, blocking collectives, on_device(): square_sum = lax.psum(jnp.sum(residual_wide * residual_wide, axis=1), 'mlp')  54.1 us
    all_gather x1, waiting for transfers between devices, on_device(): lax.all_gather(w_down.astype(jnp.bfloat16), 'req', axis=1, tiled=True)  41.2 us
    all_gather x1, blocking collectives, project_output(): lax.all_gather(weights, 'req', axis=1, tiled=True)  38 us
    unnamed x37, local copies, waits for them, and re-layouts  31.3 us
    dot_general x16, matrix products, block_step(): jnp.einsum('pthc,phcv->pthv', query_tilde, carried, precision=lax.Precisi...  27.6 us
  transfers between devices with their start and end apart: 7, of which 7 were waited for; matrix products, arithmetic and copies ran while one was open for 3% of the time, Pallas kernels for 0%

commit v1 on v0

--- a/solution.py
+++ b/solution.py
@@ -1,3 +1,4 @@
+import functools
 import jax
 import jax.numpy as jnp
 from jax import lax
@@ -5,6 +6,13 @@
 
 BLOCK = 64
 epsilon = 1e-05
+
+
+def detail_region(payload, chip_axis):
+    return lax.all_gather(payload, chip_axis).sum(axis=0)
+
+
+direct_run = functools.partial(detail_region, chip_axis="mlp")
 
 
 def add_columns(operand, weights_piece):
@@ -124,7 +132,7 @@
     ).astype(jnp.float32)
     residual = (local_rows.astype(jnp.float32) + attention).astype(jnp.bfloat16)
     residual_wide = residual.astype(jnp.float32)
-    square_sum = lax.psum(jnp.sum(residual_wide * residual_wide, axis=1), "mlp")
+    square_sum = direct_run(jnp.sum(residual_wide * residual_wide, axis=1))
     row_scale = lax.rsqrt(square_sum / model_width + epsilon)[:, None]
     gain_part = lax.dynamic_slice_in_dim(mlp_gain, offset, feature_part)
     normed_part = (residual_wide * row_scale * gain_part).astype(jnp.bfloat16)

time: 641 us -> 753 us (1.17)
  waiting for transfers between devices: 337 us -> 500 us
  blocking collectives: 92.2 us -> 38 us
    unnamed x9 -> x11, waiting for transfers between devices: 148 us -> 252 us
    all_gather x1, waiting for transfers between devices: 8.91 us -> 66.4 us  [on_device(): lax.all_gather(w_gu.astype(jnp.bfloat16), 'req', axis=0, tiled=True)]
    psum x1 -> x0, blocking collectives: 54.1 us -> none  [on_device(): square_sum = lax.psum(jnp.sum(residual_wide * residual_wide, axis=1), 'mlp')]
    unnamed x37 -> x44, local copies, waits for them, and re-layouts: 31.3 us -> 32.5 us
  transfers between devices with their start and end apart: 7 -> 8, of which waited for: 7 -> 8; matrix products, arithmetic and copies ran while one was open for 3% -> 3% of each run, Pallas kernels for 0% -> 0%
where the time goes in v1:
time: 753 us; the launch traced here: 749 us
  waiting for transfers between devices  500 us (66%)
  matrix products  121 us (16%)
  local copies, waits for them, and re-layouts  50.4 us (7%)
  blocking collectives  38 us (5%)
  other arithmetic  22.7 us (3%)
  between operations  15.1 us (2%)
    unnamed x11, waiting for transfers between devices  252 us
    all_gather x1, waiting for transfers between devices, on_device(): lax.all_gather(w_gu.astype(jnp.bfloat16), 'req', axis=0, tiled=True)  66.4 us
    all_gather x1, waiting for transfers between devices, on_device(): x_full = lax.all_gather(local_rows, 'mlp', axis=1, tiled=True)  61.3 us
    all_gather x1, waiting for transfers between devices, on_device(): normed = lax.all_gather(normed_part, 'mlp', axis=1, tiled=True)  60.9 us
    all_gather x1, waiting for transfers between devices, on_device(): lax.all_gather(w_down.astype(jnp.bfloat16), 'req', axis=1, tiled=True)  41.6 us
    all_gather x1, blocking collectives, project_output(): lax.all_gather(weights, 'req', axis=1, tiled=True)  38 us
    unnamed x44, local copies, waits for them, and re-layouts  32.5 us
    dot_general x16, matrix products, block_step(): jnp.einsum('pthc,phcv->pthv', query_tilde, carried, precision=lax.Precisi...  27.6 us
  transfers between devices with their start and end apart: 8, of which 8 were waited for; matrix products, arithmetic and copies ran while one was open for 3% of the time, Pallas kernels for 0%

profile of v1, /device:TPU:0, one launch (start us, length us, event | category | flops | bytes accessed | tf_op | source)
XLA Modules:
  0.0 748.5 jit_solution(11671130516654439487)
XLA Ops:
  7.2 1.8 convert_element_type.49
  9.1 1.5 pad_maximum_fusion
  10.7 38.0 %all_gather.26 = bf16[128,2048]{1,0:T(8,128)(2,1)} all-gather(bf16[128,256]{1,0:T(8,128)(2,1)S(1)} %convert_element_type.51), channel_id=1, replica_groups=mesh['req'=8,'mlp'=16] {'req'}, dimensions={1}, use_global_device_ids=true | all-gather | bytes 589824 | tf_op jit(solution)/shard_map/all_gather | solution.py:25
  48.7 17.4 %all-gather.9.cloned.1.call-done = bf16[2048,384]{1,0:T(8,128)(2,1)} async-done(((bf16[256,384]{1,0:T(8,128)(2,1)}), bf16[2048,384]{1,0:T(8,128)(2,1)}) %all-gather.9.cloned.1.call-update) | async-done | bytes 1572880 | tf_op jit(solution)/shard_map/all_gather | solution.py:79
  66.1 61.3 %all-gather.7.cloned.1.call-done = bf16[2052,2048]{1,0:T(8,128)(2,1)} async-done(((bf16[2052,128]{1,0:T(8,128)(2,1)}), bf16[2052,2048]{1,0:T(8,128)(2,1)}) %all-gather.7.cloned.1.call-update) | async-done | bytes 8405008 | tf_op jit(solution)/shard_map/all_gather | solution.py:76
  127.4 7.4 fusion.59
  134.9 1.6 copy-done.3
  137.3 2.2 copy-done.4
  140.8 2.6 copy.60
  144.7 108.7 %while.13 = (s32[]{:T(128)}, f32[2,1,128,128]{3,2,0,1:T(8,128)S(1)}, f32[16,2,64,1,128]{4,2,0,1,3:T(8,128)}, s32[16]{0:T(128)S(1)}, s32[2]{0:T(128)S(1)}, /*inde...) while((s32[]{:T(128)}, ...), condition=%wide.region_2.3_spmd.clone, body=%wide.region_0.2_spmd.clone.sunk | while | flops 77050048 | bytes 1596940 | solution.py:104
  148.4 1.7 fusion.93
  150.1 1.3 fusion.91
  155.2 1.7 fusion.93
  156.9 1.3 fusion.91
  162.0 1.7 fusion.93
  168.8 1.7 fusion.93
  170.5 1.3 fusion.91
  175.6 1.7 fusion.93
  177.3 1.3 fusion.91
  182.4 1.7 fusion.93
  184.1 1.3 fusion.91
  189.2 1.7 fusion.93
  196.0 1.7 fusion.93
  197.7 1.3 fusion.91
  202.8 1.7 fusion.93
  204.5 1.3 fusion.91
  209.6 1.7 fusion.93
  211.3 1.3 fusion.91
  216.4 1.7 fusion.93
  223.2 1.7 fusion.93
  229.9 1.7 fusion.93
  236.7 1.7 fusion.93
  243.5 1.7 fusion.93
  250.3 1.7 fusion.93
  254.0 1.6 fusion.49
  255.7 5.7 convolution_convert_fusion.1
  261.4 11.5 %copy.71 = bf16[2052,2048]{0,1:T(8,128)(2,1)} copy(bf16[2052,2048]{1,0:T(8,128)(2,1)} %convolution_convert_fusion.1) | data formatting | bytes 16809984
  274.8 74.0 %reduce-scatter.7.cloned.1.call-done = bf16[128,2052]{1,0:T(8,128)(2,1)} async-done(((bf16[2048,2052]{1,0:T(8,128)(2,1)}), bf16[128,2052]{1,0:T(8,128)(2,1)}) %reduce-scatter.7.cloned.1.call-update) | async-done | bytes 525328
  348.8 1.4 copy.72
  353.3 103.5 %all-reduce.3.cloned.1.call-done = f32[32832]{0:T(1024)} async-done(((f32[32832]{0:T(1024)}), f32[32832]{0:T(1024)}) %all-reduce.3.cloned.1.call-update) | async-done | bytes 131344
  460.1 66.4 %all-gather.13.cloned.1.call-done = bf16[2048,704]{0,1:T(8,128)(2,1)} async-done(((bf16[256,704]{0,1:T(8,128)(2,1)}), bf16[2048,704]{0,1:T(8,128)(2,1)}) %all-gather.13.cloned.1.call-update) | async-done | bytes 2883600 | tf_op jit(solution)/shard_map/all_gather | solution.py:141
  526.5 60.9 %all-gather.11.cloned.1.call-done = bf16[2052,2048]{1,0:T(8,128)(2,1)} async-done(((bf16[2052,128]{1,0:T(8,128)(2,1)}), bf16[2052,2048]{1,0:T(8,128)(2,1)}) %all-gather.11.cloned.1.call-update) | async-done | bytes 8405008 | tf_op jit(solution)/shard_map/all_gather | solution.py:139
  587.5 12.6 %fusion.60 = f32[2052,704]{0,1:T(8,128)} fusion(bf16[2052,2048]{1,0:T(8,128)(2,1)} %all-gather.11.cloned.1.call-done, bf16[2048,704]{0,1:T(8,128)(2,1)} %all-gather.13.cloned.1.call-done), kind=kOutput, calls=%fused_computation.85 | convolution fusion | flops 5917114368 | bytes 17067008 | tf_op jit(solution)/shard_map/dot_general | solution.py:19
  600.1 41.6 %all-gather.15.cloned.1.call-done = bf16[352,2048]{1,0:T(8,128)(2,1)} async-done(((bf16[352,256]{1,0:T(8,128)(2,1)}), bf16[352,2048]{1,0:T(8,128)(2,1)}) %all-gather.15.cloned.1.call-update) | async-done | bytes 1441808 | tf_op jit(solution)/shard_map/all_gather | solution.py:147
  641.6 11.1 %convolution_convert_fusion = bf16[2052,2048]{1,0:T(8,128)(2,1)} fusion(bf16[352,2048]{1,0:T(8,128)(2,1)} %all-gather.15.cloned.1.call-done, f32[2052,704]{0,1:T(8,128)} %fusion.60), kind=kOutput, calls=%fused_computation.48 | convolution fusion | flops 2967093504 | bytes 15625216 | tf_op jit(solution)/shard_map/dot_general | solution.py:145
  652.7 11.5 %copy.73 = bf16[2052,2048]{0,1:T(8,128)(2,1)} copy(bf16[2052,2048]{1,0:T(8,128)(2,1)} %convolution_convert_fusion) | data formatting | bytes 16809984
  664.3 74.4 %reduce-scatter.9.cloned.1.call-done = bf16[128,2052]{1,0:T(8,128)(2,1)} async-done(((bf16[2048,2052]{1,0:T(8,128)(2,1)}), bf16[128,2052]{1,0:T(8,128)(2,1)}) %reduce-scatter.9.cloned.1.call-update) | async-done | bytes 525328
  738.7 1.3 copy.74
  (250 shorter events, 82.7 us)
Async XLA Ops:
  7.2 1.9 copy-start
  7.2 3.5 copy-start.12
  7.2 58.9 %all-gather.9.cloned.1.call-start = ((), (), s32[]{:S(2)}) async-start(), calls=%async_computation.3 | async-start | bytes 1769472 | tf_op jit(solution)/shard_map/all_gather | solution.py:79
  9.0 118.4 %all-gather.7.cloned.1.call-start = ((), (), s32[]{:S(2)}) async-start(), calls=%async_computation.2 | async-start | bytes 8947712 | tf_op jit(solution)/shard_map/all_gather | solution.py:76
  10.6 338.2 %reduce-scatter.7.cloned.1.call-start = ((), (), s32[]{:S(2)}) async-start(), calls=%async_computation.8 | async-start | bytes 9469952
  134.8 1.7 copy-start.3
  136.5 0.7 copy-start.15
  137.2 2.3 copy-start.4
  137.3 3.4 copy-start.1
  143.3 1.3 slice-start
  143.3 1.3 copy-start.16
  144.7 108.8 %copy-start.11 = (f32[4,1,128,128]{3,2,1,0:T(8,128)S(1)}, f32[4,1,128,128]{3,2,1,0:T(8,128)}, u32[]{:S(2)}) copy-start(f32[4,1,128,128]{3,2,1,0:T(8,128)} %param.16) | copy-start | bytes 786436
  253.4 8.0 %copy-start.5 = (f32[2,1,128,128]{3,2,0,1:T(8,128)}, f32[2,1,128,128]{3,2,0,1:T(8,128)S(1)}, u32[]{:S(2)}) copy-start(f32[2,1,128,128]{3,2,0,1:T(8,128)S(1)} %get-tuple-element.126) | copy-start | bytes 393220
  253.4 2.3 copy-start.2
  253.4 2.3 copy-start.6
  253.4 2.3 copy-start.14
  253.6 7.8 %copy-start.7 = (f32[4,1,128,128]{3,2,1,0:T(8,128)}, f32[4,1,128,128]{3,2,1,0:T(8,128)S(1)}, u32[]{:S(2)}) copy-start(f32[4,1,128,128]{3,2,1,0:T(8,128)S(1)} %multiply_add_fusion) | copy-start | bytes 786436
  272.9 0.7 copy-start.17
  272.9 77.3 %copy-start.13 = (bf16[4,128]{1,0:T(4,128)(2,1)S(1)}, bf16[4,128]{1,0:T(4,128)(2,1)}, u32[]{:S(2)}) copy-start(bf16[4,128]{1,0:T(4,128)(2,1)} %param.14) | copy-start | bytes 3076
  272.9 183.9 %all-reduce.3.cloned.1.call-start = ((), (), s32[]{:S(2)}) async-start(), calls=%async_computation.7 | async-start | bytes 270336
  348.8 2.9 copy-start.8
  351.0 0.6 copy-start.9
  351.6 174.9 %all-gather.13.cloned.1.call-start = ((), (), s32[]{:S(2)}) async-start(), calls=%async_computation.5 | async-start | bytes 3244032 | tf_op jit(solution)/shard_map/all_gather | solution.py:141
  352.5 235.0 %all-gather.11.cloned.1.call-start = ((), (), s32[]{:S(2)}) async-start(), calls=%async_computation.4 | async-start | bytes 8947712 | tf_op jit(solution)/shard_map/all_gather | solution.py:139
  457.9 1.3 copy-start.10
  459.1 182.5 %all-gather.15.cloned.1.call-start = ((), (), s32[]{:S(2)}) async-start(), calls=%async_computation.6 | async-start | bytes 1622016 | tf_op jit(solution)/shard_map/all_gather | solution.py:147
  459.9 278.8 %reduce-scatter.9.cloned.1.call-start = ((), (), s32[]{:S(2)}) async-start(), calls=%async_computation.9 | async-start | bytes 9469952
Sparse Core Ops, SparseCore 0:
  10.9 55.1 all-gather.8
  67.7 59.6 all-gather.6
  273.1 75.6 reduce-scatter.6
  351.7 105.0 all-reduce.2
  459.7 66.8 all-gather.12
  528.1 59.3 all-gather.10
  589.9 51.6 all-gather.14
  664.4 74.2 reduce-scatter.8
